TPU v7x, 512 devices: a whole 4x8x8 slice. The times are simulated.
512 devices in a mesh: ctx: 64 (over x, z, core), head: 8 (over y).
Axes of the slice: x: 4, y: 8, z: 8, core: 2. Of those that a mesh axis runs over, the one named last changes fastest.
Arguments:
- dec_states: bfloat16 [16384, 4096], P('ctx', 'head'), may hold values from -512 to 512
- norm_gain: float32 [4096], replicated, may hold values from 0.1 to 1.9
- w_query: bfloat16 [4096, 4096], P('ctx', 'head'), may hold values from -0.09375 to 0.09375
- enc_keys: bfloat16 [131072, 4096], P('ctx', 'head'), may hold values from -128 to 128
- enc_values: bfloat16 [131072, 4096], P('ctx', 'head'), may hold values from -24 to 24
- w_out: bfloat16 [4096, 4096], P('ctx', 'head'), may hold values from -0.09375 to 0.09375
- tgt_lengths: int32 [32], replicated, may hold values from 1 to 512, 8192 in all
- src_lengths: int32 [32], replicated, may hold values from 2049 to 4096, as said below
Outputs:
- attn_output: bfloat16 [16384, 4096], P('ctx', 'head')
Inputs may be any that keep to these rules, and one draw needn't show every extreme that they name: `tgt_lengths`: the lengths sum to 8192, and the longest equals 512. `src_lengths`: every example has more than 2048 encoder rows, and some example has all 4096.
All inputs are finite; a program needn't handle non-finite values.
Results may differ from a plain program's by a relative error of at most 0.009.
Values may be sent and summed in bfloat16 or wider, within the bound.
No kernel may reach another device: no remote copies, remote signals or barrier semaphores. Data moves between devices by JAX's collectives and lax.ppermute only.
A program may use at most 64 MiB of HBM per device.

v0:
```python
import jax
import jax.numpy as jnp
from jax import lax
from jax.sharding import PartitionSpec as P

DK = 64


def partner(value, axis, distance):
    mask = 2**distance
    pairs = [(source, source ^ mask) for source in range(lax.axis_size(axis))]
    return lax.ppermute(value, axis, pairs)


def attend(queries, keys, values, key_valid):
    row_count = queries.shape[0]
    head_count = queries.shape[1] // DK
    query_heads = jnp.moveaxis(queries.reshape(row_count, head_count, DK), 1, 0)
    key_heads = jnp.moveaxis(keys.reshape(-1, head_count, DK), 1, 0)
    value_heads = jnp.moveaxis(values.reshape(-1, head_count, DK), 1, 0)

    def one_head(head_items):
        query_head, key_head, value_head = head_items
        scores = jnp.dot(query_head, key_head.T, preferred_element_type=jnp.float32)
        scores = jnp.where(key_valid[None, :], scores, -jnp.inf)
        top_score = jnp.max(scores, axis=1)
        weights = jnp.exp(scores - top_score[:, None]).astype(jnp.bfloat16)
        totals = jnp.sum(weights.astype(jnp.float32), axis=1)
        weighted = jnp.dot(weights, value_head, preferred_element_type=jnp.float32)
        return (top_score, totals, weighted)

    top_score, totals, weighted = lax.map(one_head, (query_heads, key_heads, value_heads))
    return (top_score.T, totals.T, jnp.moveaxis(weighted, 0, 1).reshape(row_count, head_count * DK))


def combine_halves(first, second):
    top_one, totals_one, weighted_one = first
    top_two, totals_two, weighted_two = second
    row_count = weighted_one.shape[0]
    head_count = top_one.shape[1]
    largest = jnp.maximum(top_one, top_two)
    scale_one = jnp.exp(top_one - largest)
    scale_two = jnp.exp(top_two - largest)
    numer = (
        weighted_one.reshape(row_count, head_count, DK) * scale_one[:, :, None]
        + weighted_two.reshape(row_count, head_count, DK) * scale_two[:, :, None]
    )
    denom = totals_one * scale_one + totals_two * scale_two
    return (numer / denom[:, :, None]).reshape(row_count, head_count * DK)


def local(dec_states, norm_gain, w_query, enc_keys, enc_values, w_out, tgt_lengths, src_lengths):
    position = lax.axis_index("ctx")
    half_index = position % 2
    example = position // 2
    slot_ids = jnp.arange(tgt_lengths.shape[0], dtype=jnp.int32)
    tgt_len = jnp.sum(jnp.where(slot_ids == example, tgt_lengths, 0))
    src_len = jnp.sum(jnp.where(slot_ids == example, src_lengths, 0))
    enc_count = enc_keys.shape[0]
    full_states = lax.all_gather(dec_states, "head", axis=1, tiled=True)
    row_count = full_states.shape[0]
    states = full_states.astype(jnp.float32)
    normed = (
        states * lax.rsqrt(jnp.mean(states * states, axis=-1, keepdims=True) + 1e-06) * norm_gain
    ).astype(jnp.bfloat16)
    columns = normed
    queries = jnp.dot(
        columns,
        lax.all_gather(w_query, "ctx", axis=0, tiled=True),
        preferred_element_type=jnp.float32,
    ).astype(jnp.bfloat16)
    offsets = jnp.arange(enc_count, dtype=jnp.int32)
    own_valid = half_index * enc_count + offsets < src_len
    far_valid = (1 - half_index) * enc_count + offsets < src_len
    far_keys, far_values = partner((enc_keys, enc_values), "ctx", 0)
    nearby = attend(queries, enc_keys, enc_values, own_valid)
    distant = attend(queries, far_keys, far_values, far_valid)
    attended = combine_halves(nearby, distant)
    live_rows = half_index * row_count + jnp.arange(row_count, dtype=jnp.int32) < tgt_len
    attended = jnp.where(live_rows[:, None], attended, 0.0).astype(jnp.bfloat16)
    all_heads = lax.all_gather(attended, "head", axis=1, tiled=True)
    columns = all_heads
    projected = jnp.dot(
        columns,
        lax.all_gather(w_out, "ctx", axis=0, tiled=True),
        preferred_element_type=jnp.float32,
    )
    return projected.astype(jnp.bfloat16)


def solution(mesh):
    placed = (
        P("ctx", "head"),
        P(),
        P("ctx", "head"),
        P("ctx", "head"),
        P("ctx", "head"),
        P("ctx", "head"),
        P(),
        P(),
    )
    return jax.shard_map(
        local, mesh=mesh, in_specs=placed, out_specs=P("ctx", "head"), check_vma=False
    )
```

profile of v0, /device:TPU:2, one launch (start us, length us, event | category | flops | bytes accessed | tf_op | source)
XLA Modules:
  0.0 284.5 jit_solution(14177036345322470178)
XLA Ops:
  6.5 0.7 all-gather.5.cloned.1.call-update
  7.3 0.7 all-gather.7.cloned.1.call-update
  8.1 2.9 %copy.11 = bf16[2048,512]{0,1:T(8,128)(2,1)S(1)} copy(bf16[2048,512]{1,0:T(8,128)(2,1)} %param.15) | data formatting | bytes 4194304 | tf_op args[3]
  11.0 1.9 collective-permute-start
  12.9 4.0 %copy.12 = bf16[2048,512]{0,1:T(8,128)(2,1)} copy(bf16[2048,512]{1,0:T(8,128)(2,1)} %param.16) | data formatting | bytes 4194304 | tf_op args[4]
  16.9 2.5 collective-permute-start.1
  19.6 0.6 fusion.38
  20.8 0.6 fusion.39
  21.5 36.2 %all-gather.5.cloned.1.call-done = bf16[256,4096]{1,0:T(8,128)(2,1)} async-done(((bf16[256,512]{1,0:T(8,128)(2,1)}), bf16[256,4096]{1,0:T(8,128)(2,1)}) %all-gather.5.cloned.1.call-update) | async-done | bytes 2097168 | tf_op jit(solution)/shard_map/all_gather | solution.py:60
  57.7 2.1 fusion.22
  59.8 84.6 %all-gather.7.cloned.1.call-done = bf16[4096,512]{1,0:T(8,128)(2,1)} async-done(((bf16[64,512]{1,0:T(8,128)(2,1)}), bf16[4096,512]{1,0:T(8,128)(2,1)}) %all-gather.7.cloned.1.call-update) | async-done | bytes 4194320 | tf_op jit(solution)/shard_map/all_gather | solution.py:69
  144.4 4.1 %fusion.29 = bf16[256,512]{1,0:T(8,128)(2,1)S(1)} fusion(bf16[4096,512]{1,0:T(8,128)(2,1)} %all-gather.7.cloned.1.call-done, bf16[256,4096]{1,0:T(8,128)(2,1)} %all-gather.5.cloned.1.call-done, f32[4096]{0:T(1024)S(1)} %copy-done.1, f32[256]{0:T(256)S(1)} %add_rsqrt_fusion), kind=kOutput, calls=%fused_computation.38 | convolution fusion | flops 1078067200 | bytes 6571008 | tf_op jit(solution)/shard_map/dot_general | solution.py:67
  149.0 32.8 %while.31 = (s32[]{:T(128)}, f32[8,256]{1,0:T(8,128)S(1)}, f32[8,256]{1,0:T(8,128)S(1)}, f32[8,256,64]{1,2,0:T(8,128)S(1)}, bf16[8,256,64]{2,1,0:T(8,128)(2,1)S(...) while((s32[]{:T(128)}, f32[8,256]{1,0:T(8,128)S(1)}, ...), condition=%wide.region_10.11_spmd.clone, body=%wide.region_7.10_spmd.clone.sunk | while | flops 138415616 | bytes 6961277 | solution.py:32
  149.0 0.6 add_compare_fusion.6
  149.6 1.4 fusion.57
  151.1 1.5 fusion.58
  153.1 0.6 add_compare_fusion.6
  153.7 1.4 fusion.57
  155.2 1.5 fusion.58
  157.2 0.6 add_compare_fusion.6
  157.8 1.5 fusion.57
  159.3 1.5 fusion.58
  161.9 1.4 fusion.57
  163.4 1.5 fusion.58
  166.0 1.4 fusion.57
  167.5 1.5 fusion.58
  170.1 1.4 fusion.57
  171.6 1.5 fusion.58
  174.2 1.4 fusion.57
  175.7 1.5 fusion.58
  178.3 1.4 fusion.57
  179.8 1.5 fusion.58
  181.8 0.8 copy-done
  182.6 25.2 %while.30 = (s32[]{:T(128)}, f32[8,256]{1,0:T(8,128)S(1)}, f32[8,256]{1,0:T(8,128)S(1)}, f32[8,256,64]{1,2,0:T(8,128)S(1)}, bf16[8,256,64]{2,1,0:T(8,128)(2,1)S(...) while((s32[]{:T(128)}, f32[8,256]{1,0:T(8,128)S(1)}, ...), condition=%wide.region_6.7_spmd.clone, body=%wide.region_3.6_spmd.clone.sunk | while | flops 138415616 | bytes 6961277 | solution.py:32
  183.8 1.5 fusion.55
  186.9 1.5 fusion.55
  190.1 1.5 fusion.55
  193.2 1.5 fusion.55
  195.2 0.6 add_compare_fusion.5
  196.4 1.5 fusion.55
  199.5 1.5 fusion.55
  202.7 1.5 fusion.55
  205.8 1.5 fusion.55
  207.9 1.1 fusion.34
  209.0 0.8 fusion.32
  209.8 19.9 %all-gather.11.cloned.1.call-done = bf16[4096,512]{1,0:T(8,128)(2,1)} async-done(((bf16[64,512]{1,0:T(8,128)(2,1)}), bf16[4096,512]{1,0:T(8,128)(2,1)}) %all-gather.11.cloned.1.call-update) | async-done | bytes 4194320 | tf_op jit(solution)/shard_map/all_gather | solution.py:85
  229.7 43.5 %all-gather.9.cloned.1.call-done = bf16[256,4096]{0,1:T(8,128)(2,1)} async-done(((bf16[256,512]{0,1:T(8,128)(2,1)}), bf16[256,4096]{0,1:T(8,128)(2,1)}) %all-gather.9.cloned.1.call-update) | async-done | bytes 2097168 | tf_op jit(solution)/shard_map/all_gather | solution.py:81
  273.1 4.8 %convolution_convert_fusion = bf16[256,512]{1,0:T(8,128)(2,1)} fusion(bf16[256,4096]{0,1:T(8,128)(2,1)} %all-gather.9.cloned.1.call-done, bf16[4096,512]{1,0:T(8,128)(2,1)} %all-gather.11.cloned.1.call-done), kind=kOutput, calls=%fused_computation.39 | convolution fusion | flops 1073872896 | bytes 6553600 | tf_op jit(solution)/shard_map/dot_general | solution.py:83
  (94 shorter events, 21.1 us)
Async XLA Ops:
  6.5 51.2 %all-gather.5.cloned.1.call-start = ((), (), s32[]{:S(2)}) async-start(), calls=%async_computation | async-start | bytes 2359296 | tf_op jit(solution)/shard_map/all_gather | solution.py:60
  7.3 137.1 %all-gather.7.cloned.1.call-start = ((), (), s32[]{:S(2)}) async-start(), calls=%async_computation.1 | async-start | bytes 4259840 | tf_op jit(solution)/shard_map/all_gather | solution.py:69
  8.0 221.6 %all-gather.11.cloned.1.call-start = ((), (), s32[]{:S(2)}) async-start(), calls=%async_computation.3 | async-start | bytes 4259840 | tf_op jit(solution)/shard_map/all_gather | solution.py:85
  11.0 8.6 %copy-start.2 = (s32[32]{0:T(128)S(1)}, s32[32]{0:T(128)}, u32[]{:S(2)}) copy-start(s32[32]{0:T(128)} %param.18) | copy-start | bytes 388
  11.0 9.8 %copy-start.3 = (s32[32]{0:T(128)S(1)}, s32[32]{0:T(128)}, u32[]{:S(2)}) copy-start(s32[32]{0:T(128)} %param.19) | copy-start | bytes 388
  11.0 137.9 %collective-permute-start = (bf16[2048,512]{0,1:T(8,128)(2,1)S(1)}, bf16[2048,512]{0,1:T(8,128)(2,1)}, u32[]{:S(2)}, u32[]{:S(2)}) collective-permute-start(bf16[2048,512]{0,1:T(8,128)(2,1)S(1)} %copy.11), channel_id=1, source_target_pairs={{0,8},{8,0},{16,24},{24,16},{32,40},{40,32},{48,56},{56,48},{64,72... | collective-permute-start | bytes 6291464 | tf_op jit(solution)/shard_map/ppermute | solution.py:12
  16.9 127.4 %copy-start.1 = (f32[4096]{0:T(1024)S(1)}, f32[4096]{0:T(1024)}, u32[]{:S(2)}) copy-start(f32[4096]{0:T(1024)} %param.13) | copy-start | bytes 49156
  16.9 132.0 %collective-permute-start.1 = (bf16[2048,512]{0,1:T(8,128)(2,1)}, bf16[2048,512]{0,1:T(8,128)(2,1)}, u32[]{:S(2)}, u32[]{:S(2)}) collective-permute-start(bf16[2048,512]{0,1:T(8,128)(2,1)} %copy.12), channel_id=1, source_target_pairs={{0,8},{8,0},{16,24},{24,16},{32,40},{40,32},{48,56},{56,48},{64,72... | collective-permute-start | bytes 6291464 | tf_op jit(solution)/shard_map/ppermute | solution.py:12
  19.5 253.7 %all-gather.9.cloned.1.call-start = ((), (), s32[]{:S(2)}) async-start(), calls=%async_computation.2 | async-start | bytes 2359296 | tf_op jit(solution)/shard_map/all_gather | solution.py:81
  181.8 0.8 copy-start
Sparse Core Ops, SparseCore 0:
  9.4 48.2 all-gather.4
  61.1 83.2 all-gather.6
  147.7 81.8 all-gather.10
  231.6 41.5 all-gather.8
where the time goes:
time: 286 us; the launch traced here: 284 us
  waiting for transfers between devices  186 us (65%)
  matrix products  48 us (17%)
  other arithmetic  22.9 us (8%)
  between operations  13.3 us (5%)
  local copies, waits for them, and re-layouts  9.49 us (3%)
  starting transfers between devices  4.57 us (2%)
    all_gather x1, waiting for transfers between devices, local(): lax.all_gather(w_query, 'ctx', axis=0, tiled=True)  84.6 us
    all_gather x1, waiting for transfers between devices, local(): all_heads = lax.all_gather(attended, 'head', axis=1, tiled=True)  43.5 us
    all_gather x1, waiting for transfers between devices, local(): full_states = lax.all_gather(dec_states, 'head', axis=1, tiled=True)  36.2 us
    dot_general x16, matrix products, one_head(): weighted = jnp.dot(weights, value_head, preferred_element_type=jnp.float32)  23.5 us
    all_gather x1, waiting for transfers between devices, local(): lax.all_gather(w_out, 'ctx', axis=0, tiled=True)  19.9 us
    dot_general x16, matrix products, one_head(): scores = jnp.dot(query_head, key_head.T, preferred_element_type=jnp.float32)  15.6 us
    unnamed x11, local copies, waits for them, and re-layouts  7.97 us
    reduce_sum x16, other arithmetic, one_head(): totals = jnp.sum(weights.astype(jnp.float32), axis=1)  6.97 us
  transfers between devices with their start and end apart: 6, of which 4 were waited for; matrix products, arithmetic and copies ran while one was open for 26% of the time, Pallas kernels for 0%

commit v1 on v0

--- a/solution.py
+++ b/solution.py
@@ -78,7 +78,16 @@
     attended = combine_halves(nearby, distant)
     live_rows = half_index * row_count + jnp.arange(row_count, dtype=jnp.int32) < tgt_len
     attended = jnp.where(live_rows[:, None], attended, 0.0).astype(jnp.bfloat16)
-    all_heads = lax.all_gather(attended, "head", axis=1, tiled=True)
+    ways = lax.axis_size("head")
+    up = [(d, (d + 1) % ways) for d in range(ways)]
+    down = [(d, (d - 1) % ways) for d in range(ways)]
+    earlier, later = ([attended], [attended])
+    for _ in range(ways // 2):
+        earlier.append(lax.ppermute(earlier[-1], "head", up))
+    for _ in range((ways - 1) // 2):
+        later.append(lax.ppermute(later[-1], "head", down))
+    line = jnp.concatenate([*earlier[::-1], *later[1:]], axis=1)
+    all_heads = jnp.roll(line, (lax.axis_index("head") - ways // 2) * attended.shape[1], axis=1)
     columns = all_heads
     projected = jnp.dot(
         columns,

time: 286 us -> 277 us (0.969)
  the two profiles are of different devices: /device:TPU:2 before, /device:TPU:32 now
where the time goes in v1:
time: 277 us; the launch traced here: 275 us
  waiting for transfers between devices  141 us (51%)
  matrix products  48 us (17%)
  starting transfers between devices  28 us (10%)
  other arithmetic  23.5 us (8%)
  local copies, waits for them, and re-layouts  21.1 us (8%)
  between operations  13.4 us (5%)
    all_gather x1, waiting for transfers between devices, local(): lax.all_gather(w_query, 'ctx', axis=0, tiled=True)  87.7 us
    all_gather x1, waiting for transfers between devices, local(): full_states = lax.all_gather(dec_states, 'head', axis=1, tiled=True)  33.7 us
    dot_general x16, matrix products, one_head(): weighted = jnp.dot(weights, value_head, preferred_element_type=jnp.float32)  23.5 us
    unnamed x26, local copies, waits for them, and re-layouts  18.8 us
    ppermute x4, waiting for transfers between devices, local(): earlier.append(lax.ppermute(earlier[-1], 'head', up))  17.9 us
    dot_general x16, matrix products, one_head(): scores = jnp.dot(query_head, key_head.T, preferred_element_type=jnp.float32)  15.6 us
    ppermute x3, starting transfers between devices, local(): later.append(lax.ppermute(later[-1], 'head', down))  15.4 us
    ppermute x4, starting transfers between devices, local(): earlier.append(lax.ppermute(earlier[-1], 'head', up))  8.22 us
  transfers between devices with their start and end apart: 12, of which 6 were waited for; matrix products, arithmetic and copies ran while one was open for 32% of the time, Pallas kernels for 0%

profile of v1, /device:TPU:32, one launch (start us, length us, event | category | flops | bytes accessed | tf_op | source)
XLA Modules:
  0.0 275.4 jit_solution(17765567889346647853)
XLA Ops:
  8.1 2.9 %copy.11 = bf16[2048,512]{0,1:T(8,128)(2,1)S(1)} copy(bf16[2048,512]{1,0:T(8,128)(2,1)} %param.15) | data formatting | bytes 4194304 | tf_op args[3]
  11.0 1.9 collective-permute-start
  13.0 4.0 %copy.12 = bf16[2048,512]{0,1:T(8,128)(2,1)} copy(bf16[2048,512]{1,0:T(8,128)(2,1)} %param.16) | data formatting | bytes 4194304 | tf_op args[4]
  16.9 2.4 collective-permute-start.1
  21.5 33.7 %all-gather.4.cloned.1.call-done = bf16[256,4096]{1,0:T(8,128)(2,1)} async-done(((bf16[256,512]{1,0:T(8,128)(2,1)}), bf16[256,4096]{1,0:T(8,128)(2,1)}) %all-gather.4.cloned.1.call-update) | async-done | bytes 2097168 | tf_op jit(solution)/shard_map/all_gather | solution.py:60
  55.2 2.1 fusion.22
  57.3 87.7 %all-gather.6.cloned.1.call-done = bf16[4096,512]{1,0:T(8,128)(2,1)} async-done(((bf16[64,512]{1,0:T(8,128)(2,1)}), bf16[4096,512]{1,0:T(8,128)(2,1)}) %all-gather.6.cloned.1.call-update) | async-done | bytes 4194320 | tf_op jit(solution)/shard_map/all_gather | solution.py:69
  145.0 4.1 %fusion.34 = bf16[256,512]{1,0:T(8,128)(2,1)S(1)} fusion(bf16[4096,512]{1,0:T(8,128)(2,1)} %all-gather.6.cloned.1.call-done, bf16[256,4096]{1,0:T(8,128)(2,1)} %all-gather.4.cloned.1.call-done, f32[4096]{0:T(1024)S(1)} %copy-done.1, f32[256]{0:T(256)S(1)} %add_rsqrt_fusion), kind=kOutput, calls=%fused_computation.41 | convolution fusion | flops 1078067200 | bytes 6571008 | tf_op jit(solution)/shard_map/dot_general | solution.py:67
  149.7 33.3 %while.31 = (s32[]{:T(128)}, f32[8,256]{1,0:T(8,128)S(1)}, f32[8,256]{1,0:T(8,128)S(1)}, f32[8,256,64]{1,2,0:T(8,128)S(1)}, bf16[8,256,64]{2,1,0:T(8,128)(2,1)S(...) while((s32[]{:T(128)}, f32[8,256]{1,0:T(8,128)S(1)}, ...), condition=%wide.region_10.11_spmd.clone, body=%wide.region_7.10_spmd.clone.sunk | while | flops 138415616 | bytes 6961277 | solution.py:32
  150.4 1.4 fusion.62
  151.8 1.5 fusion.63
  154.6 1.4 fusion.62
  156.0 1.5 fusion.63
  158.7 1.4 fusion.62
  160.2 1.5 fusion.63
  162.9 1.5 fusion.62
  164.3 1.5 fusion.63
  167.1 1.5 fusion.62
  168.5 1.5 fusion.63
  171.2 1.4 fusion.62
  172.7 1.5 fusion.63
  175.4 1.5 fusion.62
  176.8 1.5 fusion.63
  179.5 1.4 fusion.62
  181.0 1.5 fusion.63
  183.0 0.8 copy-done
  183.9 25.7 %while.30 = (s32[]{:T(128)}, f32[8,256]{1,0:T(8,128)S(1)}, f32[8,256]{1,0:T(8,128)S(1)}, f32[8,256,64]{1,2,0:T(8,128)S(1)}, bf16[8,256,64]{2,1,0:T(8,128)(2,1)S(...) while((s32[]{:T(128)}, f32[8,256]{1,0:T(8,128)S(1)}, ...), condition=%wide.region_6.7_spmd.clone, body=%wide.region_3.6_spmd.clone.sunk | while | flops 138415616 | bytes 6961277 | solution.py:32
  185.1 1.5 fusion.60
  188.3 1.5 fusion.60
  191.5 1.5 fusion.60
  194.7 1.5 fusion.60
  197.9 1.5 fusion.60
  201.2 1.5 fusion.60
  204.4 1.5 fusion.60
  207.6 1.5 fusion.60
  209.6 1.1 fusion.39
  210.8 2.5 collective-permute-start.2
  213.3 9.1 %collective-permute-done.2 = bf16[256,512]{0,1:T(8,128)(2,1)S(1)} collective-permute-done((bf16[256,512]{0,1:T(8,128)(2,1)S(1)}, bf16[256,512]{0,1:T(8,128)(2,1)S(1)}, u32[]{:S(2)}, u32[]{:S(2)}) %collective-permute-start.2) | collective-permute-done | bytes 262176 | tf_op jit(solution)/shard_map/ppermute | solution.py:86
  222.4 1.9 collective-permute-start.3
  224.3 5.1 %collective-permute-start.6 = (bf16[256,512]{0,1:T(8,128)(2,1)S(1)}, bf16[256,512]{0,1:T(8,128)(2,1)S(1)}, u32[]{:S(2)}, u32[]{:S(2)}) collective-permute-start(bf16[256,512]{0,1:T(8,128)(2,1)S(1)} %fusion.37), channel_id=1, source_target_pairs={{0,7},{1,0},{2,1},{3,2},{4,3},{5,4},{6,5},{7,6},{8,15},{9,8},{10,9... | collective-permute-start | bytes 786440 | tf_op jit(solution)/shard_map/ppermute | solution.py:88
  229.5 3.7 %collective-permute-done.3 = bf16[256,512]{0,1:T(8,128)(2,1)S(1)} collective-permute-done((bf16[256,512]{0,1:T(8,128)(2,1)S(1)}, bf16[256,512]{0,1:T(8,128)(2,1)S(1)}, u32[]{:S(2)}, u32[]{:S(2)}) %collective-permute-start.3) | collective-permute-done | bytes 262176 | tf_op jit(solution)/shard_map/ppermute | solution.py:86
  233.2 1.9 collective-permute-start.4
  235.1 5.1 %collective-permute-start.7 = (bf16[256,512]{0,1:T(8,128)(2,1)S(1)}, bf16[256,512]{0,1:T(8,128)(2,1)S(1)}, u32[]{:S(2)}, u32[]{:S(2)}) collective-permute-start(bf16[256,512]{0,1:T(8,128)(2,1)S(1)} %collective-permute-done.6), channel_id=1, source_target_pairs={{0,7},{1,0},{2,1},{3,2},{4,3},{5,4},{6,5},{7,6},{8,15},{9,8},{10,9... | collective-permute-start | bytes 786440 | tf_op jit(solution)/shard_map/ppermute | solution.py:88
  240.2 2.8 %collective-permute-done.4 = bf16[256,512]{0,1:T(8,128)(2,1)S(1)} collective-permute-done((bf16[256,512]{0,1:T(8,128)(2,1)S(1)}, bf16[256,512]{0,1:T(8,128)(2,1)S(1)}, u32[]{:S(2)}, u32[]{:S(2)}) %collective-permute-start.4) | collective-permute-done | bytes 262176 | tf_op jit(solution)/shard_map/ppermute | solution.py:86
  243.0 1.9 collective-permute-start.5
  244.9 5.1 %collective-permute-start.8 = (bf16[256,512]{0,1:T(8,128)(2,1)S(1)}, bf16[256,512]{0,1:T(8,128)(2,1)S(1)}, u32[]{:S(2)}, u32[]{:S(2)}) collective-permute-start(bf16[256,512]{0,1:T(8,128)(2,1)S(1)} %collective-permute-done.7), channel_id=1, source_target_pairs={{0,7},{1,0},{2,1},{3,2},{4,3},{5,4},{6,5},{7,6},{8,15},{9,8},{10,9... | collective-permute-start | bytes 786440 | tf_op jit(solution)/shard_map/ppermute | solution.py:88
  250.1 2.4 collective-permute-done.5
  264.1 4.8 %fusion.31 = bf16[256,512]{1,0:T(8,128)(2,1)} fusion(bf16[4096,512]{1,0:T(8,128)(2,1)} %all-gather.8.cloned.1.call-done, bf16[256,8192]{0,1:T(8,128)(2,1)} %constant_dynamic-update-slice_fusion, s32[]{:T(128)S(6)} %select_n.47), kind=kOutput, calls=%fused_computation.40 | convolution fusion | flops 1073872896 | bytes 6553604 | tf_op jit(solution)/shard_map/dot_general | solution.py:92
  (121 shorter events, 39.2 us)
Async XLA Ops:
  6.5 48.7 %all-gather.4.cloned.1.call-start = ((), (), s32[]{:S(2)}) async-start(), calls=%async_computation | async-start | bytes 2359296 | tf_op jit(solution)/shard_map/all_gather | solution.py:60
  7.3 137.8 %all-gather.6.cloned.1.call-start = ((), (), s32[]{:S(2)}) async-start(), calls=%async_computation.1 | async-start | bytes 4259840 | tf_op jit(solution)/shard_map/all_gather | solution.py:69
  8.0 11.4 %copy-start.2 = (s32[32]{0:T(128)S(1)}, s32[32]{0:T(128)}, u32[]{:S(2)}) copy-start(s32[32]{0:T(128)} %param.18) | copy-start | bytes 388
  8.0 12.8 %copy-start.3 = (s32[32]{0:T(128)S(1)}, s32[32]{0:T(128)}, u32[]{:S(2)}) copy-start(s32[32]{0:T(128)} %param.19) | copy-start | bytes 388
  8.0 256.1 %all-gather.8.cloned.1.call-start = ((), (), s32[]{:S(2)}) async-start(), calls=%async_computation.2 | async-start | bytes 4259840 | tf_op jit(solution)/shard_map/all_gather | solution.py:94
  11.0 134.0 %copy-start.1 = (f32[4096]{0:T(1024)S(1)}, f32[4096]{0:T(1024)}, u32[]{:S(2)}) copy-start(f32[4096]{0:T(1024)} %param.13) | copy-start | bytes 49156
  11.0 138.6 %collective-permute-start = (bf16[2048,512]{0,1:T(8,128)(2,1)S(1)}, bf16[2048,512]{0,1:T(8,128)(2,1)}, u32[]{:S(2)}, u32[]{:S(2)}) collective-permute-start(bf16[2048,512]{0,1:T(8,128)(2,1)S(1)} %copy.11), channel_id=1, source_target_pairs={{0,8},{8,0},{16,24},{24,16},{32,40},{40,32},{48,56},{56,48},{64,72... | collective-permute-start | bytes 6291464 | tf_op jit(solution)/shard_map/ppermute | solution.py:12
  16.9 132.7 %collective-permute-start.1 = (bf16[2048,512]{0,1:T(8,128)(2,1)}, bf16[2048,512]{0,1:T(8,128)(2,1)}, u32[]{:S(2)}, u32[]{:S(2)}) collective-permute-start(bf16[2048,512]{0,1:T(8,128)(2,1)} %copy.12), channel_id=1, source_target_pairs={{0,8},{8,0},{16,24},{24,16},{32,40},{40,32},{48,56},{56,48},{64,72... | collective-permute-start | bytes 6291464 | tf_op jit(solution)/shard_map/ppermute | solution.py:12
  183.0 0.8 copy-start
  210.8 11.6 %collective-permute-start.2 = (bf16[256,512]{0,1:T(8,128)(2,1)S(1)}, bf16[256,512]{0,1:T(8,128)(2,1)S(1)}, u32[]{:S(2)}, u32[]{:S(2)}) collective-permute-start(bf16[256,512]{0,1:T(8,128)(2,1)S(1)} %fusion.37), channel_id=1, source_target_pairs={{0,1},{1,2},{2,3},{3,4},{4,5},{5,6},{6,7},{7,0},{8,9},{9,10},{10,1... | collective-permute-start | bytes 786440 | tf_op jit(solution)/shard_map/ppermute | solution.py:86
  222.4 10.8 %collective-permute-start.3 = (bf16[256,512]{0,1:T(8,128)(2,1)S(1)}, bf16[256,512]{0,1:T(8,128)(2,1)S(1)}, u32[]{:S(2)}, u32[]{:S(2)}) collective-permute-start(bf16[256,512]{0,1:T(8,128)(2,1)S(1)} %collective-permute-done.2), channel_id=1, source_target_pairs={{0,1},{1,2},{2,3},{3,4},{4,5},{5,6},{6,7},{7,0},{8,9},{9,10},{10,1... | collective-permute-start | bytes 786440 | tf_op jit(solution)/shard_map/ppermute | solution.py:86
  224.3 10.8 %collective-permute-start.6 = (bf16[256,512]{0,1:T(8,128)(2,1)S(1)}, bf16[256,512]{0,1:T(8,128)(2,1)S(1)}, u32[]{:S(2)}, u32[]{:S(2)}) collective-permute-start(bf16[256,512]{0,1:T(8,128)(2,1)S(1)} %fusion.37), channel_id=1, source_target_pairs={{0,7},{1,0},{2,1},{3,2},{4,3},{5,4},{6,5},{7,6},{8,15},{9,8},{10,9... | collective-permute-start | bytes 786440 | tf_op jit(solution)/shard_map/ppermute | solution.py:88
  233.2 9.8 %collective-permute-start.4 = (bf16[256,512]{0,1:T(8,128)(2,1)S(1)}, bf16[256,512]{0,1:T(8,128)(2,1)S(1)}, u32[]{:S(2)}, u32[]{:S(2)}) collective-permute-start(bf16[256,512]{0,1:T(8,128)(2,1)S(1)} %collective-permute-done.3), channel_id=1, source_target_pairs={{0,1},{1,2},{2,3},{3,4},{4,5},{5,6},{6,7},{7,0},{8,9},{9,10},{10,1... | collective-permute-start | bytes 786440 | tf_op jit(solution)/shard_map/ppermute | solution.py:86
  235.1 9.8 %collective-permute-start.7 = (bf16[256,512]{0,1:T(8,128)(2,1)S(1)}, bf16[256,512]{0,1:T(8,128)(2,1)S(1)}, u32[]{:S(2)}, u32[]{:S(2)}) collective-permute-start(bf16[256,512]{0,1:T(8,128)(2,1)S(1)} %collective-permute-done.6), channel_id=1, source_target_pairs={{0,7},{1,0},{2,1},{3,2},{4,3},{5,4},{6,5},{7,6},{8,15},{9,8},{10,9... | collective-permute-start | bytes 786440 | tf_op jit(solution)/shard_map/ppermute | solution.py:88
  243.0 9.5 %collective-permute-start.5 = (bf16[256,512]{0,1:T(8,128)(2,1)S(1)}, bf16[256,512]{0,1:T(8,128)(2,1)S(1)}, u32[]{:S(2)}, u32[]{:S(2)}) collective-permute-start(bf16[256,512]{0,1:T(8,128)(2,1)S(1)} %collective-permute-done.4), channel_id=1, source_target_pairs={{0,1},{1,2},{2,3},{3,4},{4,5},{5,6},{6,7},{7,0},{8,9},{9,10},{10,1... | collective-permute-start | bytes 786440 | tf_op jit(solution)/shard_map/ppermute | solution.py:86
  244.9 12.6 %collective-permute-start.8 = (bf16[256,512]{0,1:T(8,128)(2,1)S(1)}, bf16[256,512]{0,1:T(8,128)(2,1)S(1)}, u32[]{:S(2)}, u32[]{:S(2)}) collective-permute-start(bf16[256,512]{0,1:T(8,128)(2,1)S(1)} %collective-permute-done.7), channel_id=1, source_target_pairs={{0,7},{1,0},{2,1},{3,2},{4,3},{5,4},{6,5},{7,6},{8,15},{9,8},{10,9... | collective-permute-start | bytes 786440 | tf_op jit(solution)/shard_map/ppermute | solution.py:88
Sparse Core Ops, SparseCore 0:
  9.4 45.7 all-gather.3
  58.6 86.4 all-gather.5
  148.4 81.6 all-gather.7
